TPU v7x, 32 devices: a whole 2x2x4 slice. The times are simulated.
32 devices in a mesh: sec: 8 (over z, x), row: 4 (over y, core).
Axes of the slice: x: 2, y: 2, z: 4, core: 2. Of those that a mesh axis runs over, the one named last changes fastest.
Arguments:
- left_block: bfloat16 [16, 2048, 128], P('sec', 'row'), may hold values from -6 to 6
- right_block: bfloat16 [16, 128, 2048], P('sec'), may hold values from -6 to 6
- left_ops: float32 [4, 16, 16], replicated, may hold values from -1.5 to 1.5
- right_ops: float32 [4, 16, 16], replicated, may hold values from -1.5 to 1.5
- charges: int32 [16], replicated, may hold values from 0 to 6
- live_states: int32 [16], replicated, may hold values from 64 to 128
- kept: int32 [16], replicated, may hold values from 64 to 128
- start: int32 [16, 128], replicated, may hold values from 0 to 511, all different within a row
Outputs:
- basis: float32 [16, 2048, 128], P('sec', 'row')
- right_new: float32 [16, 128, 2048], P('sec', None, 'row')
Inputs may be any that keep to these rules, and one draw needn't show every extreme that they name: The 128 start columns of a sector are distinct.
All inputs are finite; a program needn't handle non-finite values.
Results may differ from a plain program's by a relative error of at most 0.0065.
Values may be sent and summed in bfloat16 or wider, within the bound.
A program may use at most 64 MiB of HBM per device.

v0:
```python
import jax
import jax.numpy as jnp
from jax import lax
from jax.sharding import PartitionSpec as P

SITE = 16
ITERS = 2


chemical = 0.4
highest = lax.Precision.HIGHEST


def from_partner(value, axis, distance):
    mask = 2**distance
    pairs = [(source, source ^ mask) for source in range(lax.axis_size(axis))]
    return lax.ppermute(value, axis, pairs)


def gate_rows(tensor_block, operators):
    site_dim = operators.shape[1]
    grouped = tensor_block.astype(jnp.float32).reshape(
        tensor_block.shape[0] // site_dim, site_dim, tensor_block.shape[1]
    )
    mixed_rows = jnp.einsum("tij,ajk->aitk", operators, grouped, precision=highest)
    return mixed_rows.reshape(
        tensor_block.shape[0], operators.shape[0] * tensor_block.shape[1]
    ).astype(jnp.bfloat16)


def gate_columns(tensor_block, operators):
    site_dim = operators.shape[1]
    grouped = tensor_block.astype(jnp.float32).reshape(
        tensor_block.shape[0], site_dim, tensor_block.shape[1] // site_dim
    )
    mixed_columns = jnp.einsum("tij,kjb->tkib", operators, grouped, precision=highest)
    return mixed_columns.reshape(
        operators.shape[0] * tensor_block.shape[0], tensor_block.shape[1]
    ).astype(jnp.bfloat16)


def triangular_apply(factor, matrix):

    def single(lower_factor, right_side):
        return jax.scipy.linalg.solve_triangular(lower_factor, right_side.T, lower=True).T

    return jax.vmap(single)(factor, matrix)


def truncate(
    left_part, right_tensor, left_ids, right_ids, left_ops, right_ops, charges, kept, start
):
    left_gated = jax.vmap(gate_rows, in_axes=(0, None))(left_part, left_ops)
    right_gated = jax.vmap(gate_columns, in_axes=(0, None))(right_tensor, right_ops)
    weight = jnp.exp(-chemical * jnp.take(charges, right_ids).astype(jnp.float32))
    theta_block = weight[:, None, None] * jnp.einsum(
        "srk,skc->src", left_gated, right_gated, preferred_element_type=jnp.float32
    )
    columns = jnp.take(start, left_ids, axis=0)
    selector = (
        jnp.arange(left_gated.shape[2], dtype=jnp.int32)[None, :, None] == columns[:, None, :]
    ).astype(jnp.bfloat16)
    krylov = jnp.einsum("srk,skj->srj", left_gated, selector, preferred_element_type=jnp.float32)
    width_here = theta_block.shape[2] // lax.axis_size("row")
    for round_index in range(ITERS + 1):
        gram_matrix, projected = lax.psum(
            (
                jnp.einsum("sri,srj->sij", krylov, krylov, precision=highest),
                jnp.einsum("src,srj->scj", theta_block, krylov, precision=highest),
            ),
            "row",
        )
        factor = jnp.linalg.cholesky(gram_matrix)
        projected = triangular_apply(factor, projected)
        if round_index < ITERS:
            krylov = jnp.einsum("src,scj->srj", theta_block, projected, precision=highest)
    ortho_block = triangular_apply(factor, krylov)
    right_part = lax.dynamic_slice_in_dim(
        jnp.swapaxes(projected, 1, 2), lax.axis_index("row") * width_here, width_here, 2
    )
    keep_mask = (
        jnp.arange(ortho_block.shape[2], dtype=jnp.int32)[None, :]
        < jnp.take(kept, right_ids)[:, None]
    ).astype(jnp.float32)
    return (ortho_block * keep_mask[:, None, :], right_part * keep_mask[:, :, None])


def on_device(left_block, right_block, left_ops, right_ops, charges, live_states, kept, start):
    slot_count = left_block.shape[0]
    sector_count = slot_count * lax.axis_size("sec")
    top_bit = lax.axis_size("sec").bit_length() - 2
    home_ids = lax.axis_index("sec") * slot_count + jnp.arange(slot_count, dtype=jnp.int32)
    mirror_ids = (home_ids + sector_count // 2) % sector_count
    local_rows = left_block.shape[1]
    row_states = (
        lax.axis_index("row") * local_rows + jnp.arange(local_rows, dtype=jnp.int32)
    ) // SITE
    live_here = jnp.take(live_states, home_ids)
    left_masked = jnp.where(
        row_states[None, :, None] < live_here[:, None, None],
        left_block,
        jnp.zeros((), jnp.bfloat16),
    )
    arrived = from_partner(right_block, "sec", top_bit)
    ortho_block, right_part = truncate(
        left_masked, arrived, home_ids, mirror_ids, left_ops, right_ops, charges, kept, start
    )
    right_part = from_partner(right_part, "sec", top_bit)
    total_weight = lax.psum(jnp.sum(right_part * right_part), ("sec", "row"))
    return (ortho_block, right_part / jnp.sqrt(total_weight))


def solution(mesh):
    return jax.shard_map(
        on_device,
        mesh=mesh,
        in_specs=(P("sec", "row", None), P("sec", None, None), P(), P(), P(), P(), P(), P()),
        out_specs=(P("sec", "row", None), P("sec", None, "row")),
        check_vma=False,
    )
```

profile of v0, /device:TPU:0, one launch (start us, length us, event | category | flops | bytes accessed | tf_op | source)
XLA Modules:
  0.0 517.8 jit_solution(3204827785373359009)
XLA Ops:
  7.2 4.1 collective-permute-start
  14.0 1.7 fusion.15
  18.5 1.7 fusion.40
  20.2 37.1 %collective-permute-done = bf16[2,128,2048]{2,1,0:T(8,128)(2,1)S(1)} collective-permute-done((bf16[2,128,2048]{2,1,0:T(8,128)(2,1)}, bf16[2,128,2048]{2,1,0:T(8,128)(2,1)S(1)}, u32[]{:S(2)}, u32[]{:S(2)}) %collective-permute-start) | collective-permute-done | bytes 1048608 | tf_op jit(solution)/shard_map/ppermute | solution.py:17
  57.5 3.6 convert_bitcast_fusion
  61.1 2.7 copy.37
  63.8 7.3 %convert_element_type.41 = bf16[2,512,2048]{2,1,0:T(8,128)(2,1)} reshape(bf16[2,4,128,16,128]{4,3,2,1,0:T(8,128)(2,1)} %copy.37) | data formatting | bytes 8388608 | tf_op jit(solution)/shard_map/vmap()/convert_element_type | solution.py:39
  71.1 4.6 fusion.39
  75.7 3.2 copy-done.3
  78.9 6.4 %fusion.8 = f32[2,128,2048]{2,1,0:T(8,128)} fusion(f32[2,512,128]{2,1,0:T(8,128)S(1)} %fusion.17, f32[2,512,2048]{2,1,0:T(8,128)S(1)} %fusion.39, f32[2]{0:T(128)S(1)} %fusion.38), kind=kOutput, calls=%fused_computation.12 | convolution fusion | flops 3223322624 | bytes 11010056 | tf_op jit(solution)/shard_map/src,srj->scj/dot_general | solution.py:69
  85.4 54.8 %all-reduce.11.cloned.1.call-done = (f32[2,128,2048]{2,1,0:T(8,128)}, f32[2,128,128]{1,2,0:T(8,128)}) async-done(((f32[2,128,2048]{2,1,0:T(8,128)}, f32[2,128,128]{1,2,0:T(8,128)}), (f32[2,128,2048]{2,1,0:T(8,128)}, f32[2,128,128]{1,2,0:T(8,128)})) %all-reduce.11.cloned.1.call-update) | async-done | bytes 2228240 | tf_op jit(solution)/shard_map/psum | solution.py:66
  142.1 23.7 %custom-call.15 = f32[2,128,128]{2,1,0:T(8,128)S(1)} custom-call(f32[2,128,128]{2,1,0:T(8,128)S(1)} %fusion.28), custom_call_target="Cholesky" | custom-call | tf_op jit(solution)/shard_map/jit(cholesky)/cholesky | solution.py:73
  166.1 19.7 %custom-call.16 = f32[2,1,128,128]{2,3,1,0:T(8,128)S(1)} custom-call(f32[2,1,128,128]{3,2,1,0:T(8,128)S(1)} %select_bitcast_fusion.1), custom_call_target="InvertDiagBlocksLowerTriangular" | custom-call | tf_op jit(solution)/shard_map/vmap(jit(_solve_triangular))/triangular_solve | solution.py:45
  185.8 3.7 fusion.26
  189.4 21.6 %fusion.6 = f32[2,512,128]{2,1,0:T(8,128)S(1)} fusion(f32[2,128,2048]{2,1,0:T(8,128)S(1)} %fusion.26, f32[2,512,2048]{2,1,0:T(8,128)} %copy-done.3, f32[2]{0:T(128)S(1)} %fusion.38), kind=kOutput, calls=%fused_computation.10 | convolution fusion | flops 3223322624 | bytes 11010056 | tf_op jit(solution)/shard_map/src,scj->srj/dot_general | solution.py:76
  211.0 6.4 %fusion.4 = f32[2,128,2048]{2,1,0:T(8,128)} fusion(f32[2,512,128]{2,1,0:T(8,128)S(1)} %fusion.6, f32[2,512,2048]{2,1,0:T(8,128)S(1)} %bitcast.84, f32[2]{0:T(128)S(1)} %fusion.38), kind=kOutput, calls=%fused_computation.8 | convolution fusion | flops 3223322624 | bytes 11010056 | tf_op jit(solution)/shard_map/src,srj->scj/dot_general | solution.py:69
  217.4 1.7 fusion.41
  219.2 53.7 %all-reduce.9.cloned.1.call-done = (f32[2,128,2048]{2,1,0:T(8,128)}, f32[2,128,128]{1,2,0:T(8,128)}) async-done(((f32[2,128,2048]{2,1,0:T(8,128)}, f32[2,128,128]{1,2,0:T(8,128)}), (f32[2,128,2048]{2,1,0:T(8,128)}, f32[2,128,128]{1,2,0:T(8,128)})) %all-reduce.9.cloned.1.call-update) | async-done | bytes 2228240 | tf_op jit(solution)/shard_map/psum | solution.py:66
  274.8 23.5 %custom-call.17 = f32[2,128,128]{2,1,0:T(8,128)S(1)} custom-call(f32[2,128,128]{2,1,0:T(8,128)S(1)} %fusion.25), custom_call_target="Cholesky" | custom-call | tf_op jit(solution)/shard_map/jit(cholesky)/cholesky | solution.py:73
  298.5 19.7 %custom-call.18 = f32[2,1,128,128]{2,3,1,0:T(8,128)S(1)} custom-call(f32[2,1,128,128]{3,2,1,0:T(8,128)S(1)} %select_bitcast_fusion), custom_call_target="InvertDiagBlocksLowerTriangular" | custom-call | tf_op jit(solution)/shard_map/vmap(jit(_solve_triangular))/triangular_solve | solution.py:45
  318.2 3.7 fusion.23
  321.9 9.5 %fusion.2 = f32[2,512,128]{2,1,0:T(8,128)S(1)} fusion(f32[2,128,2048]{2,1,0:T(8,128)S(1)} %fusion.23, f32[2,512,2048]{2,1,0:T(8,128)} %copy-done.3, f32[2]{0:T(128)S(1)} %fusion.38), kind=kOutput, calls=%fused_computation.6 | convolution fusion | flops 3223322624 | bytes 11010056 | tf_op jit(solution)/shard_map/src,scj->srj/dot_general | solution.py:76
  331.4 6.4 %fusion = f32[2,128,2048]{2,1,0:T(8,128)} fusion(f32[2,512,128]{2,1,0:T(8,128)S(1)} %fusion.2, f32[2,512,2048]{2,1,0:T(8,128)S(1)} %bitcast.86, f32[2]{0:T(128)S(1)} %fusion.38), kind=kOutput, calls=%fused_computation.4 | convolution fusion | flops 3223322624 | bytes 11010056 | tf_op jit(solution)/shard_map/src,srj->scj/dot_general | solution.py:69
  337.8 1.7 fusion.42
  340.3 53.0 %all-reduce.7.cloned.1.call-done = (f32[2,128,128]{1,2,0:T(8,128)}, f32[2,128,2048]{2,1,0:T(8,128)}) async-done(((f32[2,128,128]{1,2,0:T(8,128)}, f32[2,128,2048]{2,1,0:T(8,128)}), (f32[2,128,128]{1,2,0:T(8,128)}, f32[2,128,2048]{2,1,0:T(8,128)})) %all-reduce.7.cloned.1.call-update) | async-done | bytes 2228240 | tf_op jit(solution)/shard_map/psum | solution.py:66
  395.2 23.5 %custom-call.19 = f32[2,128,128]{2,1,0:T(8,128)S(1)} custom-call(f32[2,128,128]{2,1,0:T(8,128)S(1)} %fusion.22), custom_call_target="Cholesky" | custom-call | tf_op jit(solution)/shard_map/jit(cholesky)/cholesky | solution.py:73
  418.9 19.9 %custom-call.10 = f32[2,1,128,128]{2,3,1,0:T(8,128)S(1)} custom-call(f32[2,1,128,128]{3,2,1,0:T(8,128)S(1)} %fusion.29), custom_call_target="InvertDiagBlocksLowerTriangular" | custom-call | tf_op jit(solution)/shard_map/vmap(jit(_solve_triangular))/triangular_solve | solution.py:45
  438.9 3.5 fusion.19
  442.5 2.5 collective-permute-start.1
  445.0 23.2 %collective-permute-done.1 = f32[2,128,512]{2,1,0:T(8,128)S(1)} collective-permute-done((f32[2,128,512]{2,1,0:T(8,128)S(1)}, f32[2,128,512]{2,1,0:T(8,128)S(1)}, u32[]{:S(2)}, u32[]{:S(2)}) %collective-permute-start.1) | collective-permute-done | bytes 524320 | tf_op jit(solution)/shard_map/ppermute | solution.py:17
  468.9 1.4 convolution_multiply_fusion
  470.3 39.0 %psum.55 = f32[]{:T(128)} all-reduce(f32[]{:T(128)} %multiply_reduce_fusion), channel_id=1, replica_groups=mesh['sec'=8,'row'=4] {'sec','row'}, use_global_device_ids=true, to_apply=%region_9.13 | all-reduce | flops 1 | bytes 8 | tf_op jit(solution)/shard_map/psum | solution.py:109
  (67 shorter events, 14.7 us)
Async XLA Ops:
  7.2 50.3 %copy-start = (f32[4,16,16]{2,1,0:T(8,128)S(1)}, f32[4,16,16]{2,1,0:T(8,128)}, u32[]{:S(2)}) copy-start(f32[4,16,16]{2,1,0:T(8,128)} %param.16) | copy-start | bytes 12292
  7.2 9.5 %copy-start.4 = (s32[16,128]{1,0:T(8,128)S(1)}, s32[16,128]{1,0:T(8,128)}, u32[]{:S(2)}) copy-start(s32[16,128]{1,0:T(8,128)} %param.20) | copy-start | bytes 24580
  7.2 10.1 %copy-start.1 = (s32[16]{0:T(128)S(1)}, s32[16]{0:T(128)}, u32[]{:S(2)}) copy-start(s32[16]{0:T(128)} %param.17) | copy-start | bytes 196
  7.2 133.0 %all-reduce.11.cloned.1.call-start = ((), (), s32[]{:S(2)}) async-start(), calls=%async_computation.2 | async-start | bytes 4456448 | tf_op jit(solution)/shard_map/psum | solution.py:66
  7.2 50.0 %collective-permute-start = (bf16[2,128,2048]{2,1,0:T(8,128)(2,1)}, bf16[2,128,2048]{2,1,0:T(8,128)(2,1)S(1)}, u32[]{:S(2)}, u32[]{:S(2)}) collective-permute-start(bf16[2,128,2048]{2,1,0:T(8,128)(2,1)} %param.14), channel_id=1, source_target_pairs={{0,16},{4,20},{8,24},{12,28},{16,0},{20,4},{24,8},{28,12},{1,17},{... | collective-permute-start | bytes 3145736 | tf_op jit(solution)/shard_map/ppermute | solution.py:17
  75.7 3.2 copy-start.3
  85.3 187.6 %all-reduce.9.cloned.1.call-start = ((), (), s32[]{:S(2)}) async-start(), calls=%async_computation.1 | async-start | bytes 4456448 | tf_op jit(solution)/shard_map/psum | solution.py:66
  185.8 25.3 %slice-start = ((s8[8388608]{0:T(1024)(128)(4,1)}), s8[4194304]{0:T(1024)(128)(4,1)S(1)}, s32[]{:S(2)}) async-start(s8[8388608]{0:T(1024)(128)(4,1)} %bitcast.83), calls=%async_computation.3 | async-start | bytes 8388608
  189.4 21.6 %slice-start.1 = ((s8[8388608]{0:T(1024)(128)(4,1)}), s8[4194304]{0:T(1024)(128)(4,1)S(1)}, s32[]{:S(2)}) async-start(s8[8388608]{0:T(1024)(128)(4,1)} %bitcast.83), calls=%async_computation.4 | async-start | bytes 8388608
  219.1 174.2 %all-reduce.7.cloned.1.call-start = ((), (), s32[]{:S(2)}) async-start(), calls=%async_computation | async-start | bytes 4456448 | tf_op jit(solution)/shard_map/psum | solution.py:66
  318.2 13.2 %slice-start.2 = ((s8[8388608]{0:T(1024)(128)(4,1)}), s8[4194304]{0:T(1024)(128)(4,1)S(1)}, s32[]{:S(2)}) async-start(s8[8388608]{0:T(1024)(128)(4,1)} %bitcast.85), calls=%async_computation.5 | async-start | bytes 8388608
  321.9 9.5 %slice-start.3 = ((s8[8388608]{0:T(1024)(128)(4,1)}), s8[4194304]{0:T(1024)(128)(4,1)S(1)}, s32[]{:S(2)}) async-start(s8[8388608]{0:T(1024)(128)(4,1)} %bitcast.85), calls=%async_computation.6 | async-start | bytes 8388608
  331.4 8.1 %copy-start.2 = (s32[16]{0:T(128)S(1)}, s32[16]{0:T(128)}, u32[]{:S(2)}) copy-start(s32[16]{0:T(128)} %param.19) | copy-start | bytes 196
  442.5 25.6 %collective-permute-start.1 = (f32[2,128,512]{2,1,0:T(8,128)S(1)}, f32[2,128,512]{2,1,0:T(8,128)S(1)}, u32[]{:S(2)}, u32[]{:S(2)}) collective-permute-start(f32[2,128,512]{2,1,0:T(8,128)S(1)} %dynamic-slice_multiply_fusion), channel_id=1, source_target_pairs={{0,16},{4,20},{8,24},{12,28},{16,0},{20,4},{24,8},{28,12},{1,17},{... | collective-permute-start | bytes 1572872 | tf_op jit(solution)/shard_map/ppermute | solution.py:17
Sparse Core Ops, SparseCore 0:
  85.4 54.7 all-reduce.10
  219.2 53.5 all-reduce.8
  339.6 53.5 all-reduce.6
where the time goes:
time: 527 us; the launch traced here: 518 us
  waiting for transfers between devices  222 us (42%)
  other arithmetic  137 us (26%)
  matrix products  77.8 us (15%)
  blocking collectives  39 us (7%)
  local copies, waits for them, and re-layouts  20.6 us (4%)
  between operations  15.3 us (3%)
  starting transfers between devices  6.72 us (1%)
    psum x3, waiting for transfers between devices, truncate(): lax.psum((jnp.einsum('sri,srj->sij', krylov, krylov, precision=highest),...  161 us
    another operation x10, other arithmetic, truncate(): factor = jnp.linalg.cholesky(gram_matrix)  71.1 us
    ppermute x2, waiting for transfers between devices, from_partner(): return lax.ppermute(value, axis, pairs)  60.2 us
    another operation x7, other arithmetic, single(): jax.scipy.linalg.solve_triangular(lower_factor, right_side.T, lower=True)  59.6 us
    psum x1, blocking collectives, on_device(): total_weight = lax.psum(jnp.sum(right_part * right_part), ('sec', 'row'))  39 us
    dot_general x2, matrix products, truncate(): jnp.einsum('src,scj->srj', theta_block, projected, precision=highest)  31.1 us
    dot_general x3, matrix products, truncate(): jnp.einsum('src,srj->scj', theta_block, krylov, precision=highest)  19.1 us
    another operation x4, matrix products, single(): jax.scipy.linalg.solve_triangular(lower_factor, right_side.T, lower=True)  12.2 us
  transfers between devices with their start and end apart: 5, of which 5 were waited for; matrix products, arithmetic and copies ran while one was open for 2% of the time, Pallas kernels for 0%

commit v1 on v0

v1 whole, which is shorter than its diff:
```python
import functools

import jax
import jax.numpy as jnp
from jax import lax
from jax.experimental import pallas as pl
from jax.experimental.pallas import tpu as pltpu
from jax.sharding import PartitionSpec as P

MESH = pl.DeviceIdType.MESH
HIGHEST = lax.Precision.HIGHEST
F32, BF16 = jnp.float32, jnp.bfloat16
chemical = 0.4
ITERS = 2
PANEL = 16
VM = pl.BlockSpec(memory_space=pltpu.VMEM)
SM = pl.BlockSpec(memory_space=pltpu.SMEM)


def nn(a, b, precision=None):
    return lax.dot_general(
        a, b, (((1,), (0,)), ((), ())), precision=precision, preferred_element_type=F32
    )


def nt(a, b, precision=None):
    return lax.dot_general(
        a, b, (((1,), (1,)), ((), ())), precision=precision, preferred_element_type=F32
    )


def tn(a, b, precision=None):
    return lax.dot_general(
        a, b, (((0,), (0,)), ((), ())), precision=precision, preferred_element_type=F32
    )


def split2(x):
    high = x.astype(BF16)
    return high, (x - high.astype(F32)).astype(BF16)


def split3(x):
    high, rest = x.astype(BF16), None
    rest = x - high.astype(F32)
    mid = rest.astype(BF16)
    return high, mid, (rest - mid.astype(F32)).astype(BF16)


def iota(shape, dim):
    return lax.broadcasted_iota(jnp.int32, shape, dim)


def exchange_kernel(row_count, mask, left_ref, right_ref, left_out, right_out, send, recv):
    row, sec = lax.axis_index("row"), lax.axis_index("sec")
    rows = left_ref.shape[1]
    depth = right_ref.shape[1] // row_count

    def peer_row(distance):
        return (sec, jnp.bitwise_xor(row, distance))

    partner = (jnp.bitwise_xor(sec, mask), row)
    distances = []
    step = row_count // 2
    while step:
        distances.append(step)
        step //= 2
    barrier = pltpu.get_barrier_semaphore()
    for device in [partner] + [peer_row(d) for d in distances]:
        pl.semaphore_signal(barrier, inc=1, device_id=device, device_id_type=MESH)
    pl.semaphore_wait(barrier, 1 + len(distances))

    def left_at(owner):
        return left_out.at[:, pl.ds(pl.multiple_of(owner * rows, rows), rows), :]

    def right_at(ref, owner):
        return ref.at[:, pl.ds(pl.multiple_of(owner * depth, depth), depth), :]

    copies = []

    def go(source, target, device):
        index = len(copies)
        copy = pltpu.make_async_remote_copy(
            src_ref=source, dst_ref=target, send_sem=send.at[index], recv_sem=recv.at[index],
            device_id=device, device_id_type=MESH,
        )
        copy.start()
        copies.append(copy)
        return copy

    taken = []

    def arrive(copy):
        if copy is not None and id(copy) not in taken:
            copy.wait_recv()
            taken.append(id(copy))

    first = go(right_at(right_ref, row), right_at(right_out, row), partner)
    held = [(row, None)]
    for distance in distances:
        sent = []
        for owner, copy in held:
            arrive(copy)
            source = left_ref if copy is None else left_at(owner)
            sent.append(
                (jnp.bitwise_xor(owner, distance), go(source, left_at(owner), peer_row(distance)))
            )
        held = held + sent
    own = pl.ds(pl.multiple_of(row * rows, rows), rows)
    left_out[:, own, :] = left_ref[...]
    held = [(row, first)]
    for distance in distances:
        sent = []
        for owner, copy in held:
            arrive(copy)
            block = right_at(right_out, owner)
            sent.append((jnp.bitwise_xor(owner, distance), go(block, block, peer_row(distance))))
        held = held + sent
    for copy in copies:
        copy.wait_send()
        arrive(copy)


def exchange(row_count, sec_count, left, right):
    slots, rows, states = left.shape
    count = 2 * (row_count - 1) + 1
    return pl.pallas_call(
        functools.partial(exchange_kernel, row_count, sec_count // 2),
        out_shape=(
            jax.ShapeDtypeStruct((slots, rows * row_count, states), left.dtype),
            jax.ShapeDtypeStruct(right.shape, right.dtype),
        ),
        in_specs=[VM] * 2,
        out_specs=[VM] * 2,
        scratch_shapes=[pltpu.SemaphoreType.DMA((count,)), pltpu.SemaphoreType.DMA((count,))],
        compiler_params=pltpu.CompilerParams(collective_id=0, has_side_effects=True),
    )(left, right)


def spread(ops, row_of, col_of, same):
    site = ops.shape[0]
    pick_rows = (iota((row_of.shape[0], site), 1) == row_of).astype(BF16)
    pick_cols = (iota((site, col_of.shape[1]), 0) == col_of).astype(BF16)
    out = []
    for part in split2(ops):
        wide = nn(nn(pick_rows, part).astype(BF16), pick_cols)
        out.append(jnp.where(same, wide, 0.0).astype(BF16))
    return out


def inverse_factor(grams, s_ref, t_ref):
    size = grams[0].shape[0]
    slots = len(grams)
    eye = (iota((size, size), 0) == iota((size, size), 1)).astype(F32)
    for s in range(slots):
        s_ref[s] = grams[s]
        t_ref[s] = eye
    sub = iota((PANEL, size), 0)
    lane = iota((PANEL, size), 1)

    def panel(p, carry):
        base = pl.multiple_of(p * PANEL, PANEL)
        for s in range(slots):
            upper = s_ref[s, pl.ds(base, PANEL), :]
            lower = t_ref[s, pl.ds(base, PANEL), :]
            turned = pltpu.roll(upper, lax.rem(size - base, size), 1)
            cols = [jnp.broadcast_to(turned[:, c : c + 1], (PANEL, size)) for c in range(PANEL)]
            for j in range(PANEL):
                scale = lax.rsqrt(cols[j][j : j + 1, :])
                below = jnp.where(sub > j, cols[j] * scale, 0.0)
                at_j = sub == j

                def eliminate(x):
                    pivot = x[j : j + 1, :] * scale
                    return jnp.where(at_j, pivot, x - below * pivot)

                upper, lower = eliminate(upper), eliminate(lower)
                cols = [eliminate(c) if i > j else c for i, c in enumerate(cols)]
            t_ref[s, pl.ds(base, PANEL), :] = lower
            u3, l3 = split3(upper), split3(lower)
            later = lane >= base + PANEL
            m3 = [jnp.where(later, x.astype(F32), 0.0).astype(BF16) for x in u3]
            pairs = ((0, 0), (0, 1), (1, 0), (1, 1), (0, 2), (2, 0))
            lhs = jnp.concatenate([m3[i] for i, _ in pairs], axis=0)
            rhs = jnp.concatenate(
                [jnp.concatenate([u3[k], l3[k]], axis=1) for _, k in pairs], axis=0
            )
            change = tn(lhs, rhs)
            s_ref[s] = s_ref[s] - change[:, :size]
            t_ref[s] = t_ref[s] - change[:, size:]
        return carry

    lax.fori_loop(0, size // PANEL, panel, 0)


def chain_kernel(
    sector_count, left_ref, right_ref, lops_ref, rops_ref, charges_ref, live_ref, kept_ref,
    start_ref, m_out, u_out, part_out, at_ref, b_ref, kl_ref, kr_ref, ga_ref, gb_ref, s_ref,
    t_ref,
):
    slots, rows, states = left_ref.shape
    terms, site = lops_ref.shape[0], lops_ref.shape[1]
    cols = right_ref.shape[2]
    width = cols // site
    group = 256 // site
    block = group * site
    sec, row = lax.axis_index("sec"), lax.axis_index("row")
    homes = [sec * slots + s for s in range(slots)]
    mirrors = [lax.rem(h + sector_count // 2, sector_count) for h in homes]
    r0, c0 = iota((block, 1), 0), iota((1, block), 1)
    for t in range(terms):
        parts = spread(lops_ref[t].T, r0 % site, c0 % site, (r0 // site) == (c0 // site))
        for h in range(2):
            kl_ref[h, :, t * block : (t + 1) * block] = parts[h]
        parts = spread(rops_ref[t], r0 // group, c0 // group, (r0 % group) == (c0 % group))
        for h in range(2):
            kr_ref[h, t * block : (t + 1) * block, :] = parts[h]
    for s in range(slots):
        limit = live_ref[homes[s]] * site

        def left_chunk(c, carry):
            base = pl.multiple_of(c * block, block)
            piece = left_ref[s, pl.ds(base, block), :]
            piece = jnp.where(iota((block, states), 0) + base < limit, piece.astype(F32), 0.0)
            turned = piece.T.astype(BF16)
            out = nn(turned, kl_ref[0]) + nn(turned, kl_ref[1])
            for t in range(terms):
                at_ref[s, t * states : (t + 1) * states, pl.ds(base, block)] = out[
                    :, t * block : (t + 1) * block
                ].astype(BF16)
            return carry

        lax.fori_loop(0, rows // block, left_chunk, 0)

        def right_chunk(c, carry):
            base = pl.multiple_of(c * group, group)
            piece = right_ref[s, pl.ds(base, group), :]
            stack = jnp.concatenate([piece[:, j * width : (j + 1) * width] for j in range(site)], axis=0)
            out = (nn(kr_ref[0], stack) + nn(kr_ref[1], stack)).astype(BF16)
            for t in range(terms):
                for i in range(site):
                    b_ref[
                        s, pl.ds(t * states + base, group), i * width : (i + 1) * width
                    ] = out[t * block + i * group : t * block + (i + 1) * group, :]
            return carry

        lax.fori_loop(0, states // group, right_chunk, 0)
        ga_ref[s] = nt(at_ref[s], at_ref[s])
        gb_ref[s] = nt(b_ref[s], b_ref[s])

    bond = terms * states
    weights = [
        jnp.exp(jnp.full((1, states), charges_ref[m], jnp.int32).astype(F32) * (-chemical))
        for m in mirrors
    ]
    coef = []
    for s in range(slots):
        wanted = start_ref[pl.ds(homes[s], 1), :]
        coef.append((iota((bond, wanted.shape[1]), 0) == wanted).astype(F32))
    for round_index in range(ITERS + 1):
        image = [nn(ga_ref[s], coef[s], HIGHEST) for s in range(slots)]
        inverse_factor([tn(coef[s], image[s], HIGHEST) for s in range(slots)], s_ref, t_ref)
        image = [nt(image[s], t_ref[s], HIGHEST) for s in range(slots)]
        if round_index < ITERS:
            coef = [
                nn(gb_ref[s], image[s], HIGHEST) * (weights[s] * weights[s]) for s in range(slots)
            ]
        else:
            coef = [nt(coef[s], t_ref[s], HIGHEST) for s in range(slots)]
    local_rows = u_out.shape[1]
    total = jnp.zeros((8, states), F32)
    for s in range(slots):
        keep = iota((bond, coef[s].shape[1]), 1) < kept_ref[mirrors[s]]
        out = jnp.where(keep, image[s] * weights[s], 0.0)
        m_out[s] = out.astype(BF16)
        per = out * nn(gb_ref[s], out, HIGHEST)
        total = total + jnp.sum(per.reshape(bond // 8, 8, per.shape[1]), axis=0)
        high, low = split2(jnp.where(keep, coef[s], 0.0))
        here = at_ref[s, :, pl.ds(pl.multiple_of(row * local_rows, local_rows), local_rows)]
        u_out[s] = tn(here, high) + tn(here, low)
    part_out[...] = total


def chain(sector_count, left, right, lops, rops, charges, live, kept, start, local_rows):
    slots, rows, states = left.shape
    terms, site = lops.shape[0], lops.shape[1]
    cols, bond, keep = right.shape[2], terms * states, start.shape[1]
    block = 256
    return pl.pallas_call(
        functools.partial(chain_kernel, sector_count),
        out_shape=(
            jax.ShapeDtypeStruct((slots, bond, keep), BF16),
            jax.ShapeDtypeStruct((slots, local_rows, keep), F32),
            jax.ShapeDtypeStruct((8, keep), F32),
        ),
        in_specs=[VM] * 4 + [SM] * 3 + [VM],
        out_specs=[VM] * 3,
        scratch_shapes=[
            pltpu.VMEM((slots, bond, rows), BF16),
            pltpu.VMEM((slots, bond, cols), BF16),
            pltpu.VMEM((2, block, terms * block), BF16),
            pltpu.VMEM((2, terms * block, block), BF16),
            pltpu.VMEM((slots, bond, bond), F32),
            pltpu.VMEM((slots, bond, bond), F32),
            pltpu.VMEM((slots, keep, keep), F32),
            pltpu.VMEM((slots, keep, keep), F32),
        ],
        compiler_params=pltpu.CompilerParams(vmem_limit_bytes=56 * 2**20),
    )(left, right, lops, rops, charges, live, kept, start)


def deliver_kernel(sec_count, m_ref, part_ref, m_out, parts_out, m_send, m_recv, send, recv):
    row, sec = lax.axis_index("row"), lax.axis_index("sec")
    partner = (jnp.bitwise_xor(sec, sec_count // 2), row)
    barrier = pltpu.get_barrier_semaphore()
    for d in range(1, sec_count):
        pl.semaphore_signal(
            barrier, inc=1, device_id=(jnp.bitwise_xor(sec, d), row), device_id_type=MESH
        )
    pl.semaphore_wait(barrier, sec_count - 1)
    small = []
    for d in range(1, sec_count):
        copy = pltpu.make_async_remote_copy(
            src_ref=part_ref, dst_ref=parts_out.at[d], send_sem=send.at[d], recv_sem=recv.at[d],
            device_id=(jnp.bitwise_xor(sec, d), row), device_id_type=MESH,
        )
        copy.start()
        small.append(copy)
    big = pltpu.make_async_remote_copy(
        src_ref=m_ref, dst_ref=m_out, send_sem=m_send, recv_sem=m_recv, device_id=partner,
        device_id_type=MESH,
    )
    big.start()
    parts_out[0] = part_ref[...]
    for copy in small:
        copy.wait()
    big.wait()


def deliver(sec_count, m, part):
    return pl.pallas_call(
        functools.partial(deliver_kernel, sec_count),
        out_shape=(
            jax.ShapeDtypeStruct(m.shape, m.dtype),
            jax.ShapeDtypeStruct((sec_count,) + part.shape, part.dtype),
        ),
        in_specs=[VM] * 2,
        out_specs=[VM] * 2,
        scratch_shapes=[
            pltpu.SemaphoreType.DMA,
            pltpu.SemaphoreType.DMA,
            pltpu.SemaphoreType.DMA((sec_count,)),
            pltpu.SemaphoreType.DMA((sec_count,)),
        ],
        compiler_params=pltpu.CompilerParams(collective_id=1, has_side_effects=True),
    )(m, part)


def finish_kernel(row_count, m_ref, parts_ref, right_ref, rops_ref, out_ref, kr_ref, b_ref):
    slots, states, cols = right_ref.shape
    terms, site = rops_ref.shape[0], rops_ref.shape[1]
    width = cols // site
    group = 256 // site
    block = group * site
    here = site // row_count
    part_rows = here * group
    row = lax.axis_index("row")
    r0, c0 = iota((part_rows, 1), 0), iota((1, block), 1)
    for t in range(terms):
        parts = spread(
            rops_ref[t], row * here + r0 // group, c0 // group, (r0 % group) == (c0 % group)
        )
        for h in range(2):
            kr_ref[h, t * part_rows : (t + 1) * part_rows, :] = parts[h]
    total = jnp.sum(jnp.sum(parts_ref[...], axis=0), keepdims=True)
    scale = 1.0 / jnp.sqrt(total)
    for s in range(slots):
        def right_chunk(c, carry):
            base = pl.multiple_of(c * group, group)
            piece = right_ref[s, pl.ds(base, group), :]
            stack = jnp.concatenate([piece[:, j * width : (j + 1) * width] for j in range(site)], axis=0)
            out = (nn(kr_ref[0], stack) + nn(kr_ref[1], stack)).astype(BF16)
            for t in range(terms):
                for i in range(here):
                    b_ref[pl.ds(t * states + base, group), i * width : (i + 1) * width] = out[
                        t * part_rows + i * group : t * part_rows + (i + 1) * group, :
                    ]
            return carry

        lax.fori_loop(0, states // group, right_chunk, 0)
        out_ref[s] = tn(m_ref[s], b_ref[...]) * scale


def finish(row_count, m, parts, right, rops):
    slots, states, cols = right.shape
    terms, site = rops.shape[0], rops.shape[1]
    return pl.pallas_call(
        functools.partial(finish_kernel, row_count),
        out_shape=jax.ShapeDtypeStruct((slots, m.shape[2], cols // row_count), F32),
        in_specs=[VM] * 4,
        out_specs=VM,
        scratch_shapes=[
            pltpu.VMEM((2, terms * 256 // row_count, 256), BF16),
            pltpu.VMEM((terms * states, cols // row_count), BF16),
        ],
        compiler_params=pltpu.CompilerParams(vmem_limit_bytes=40 * 2**20),
    )(m, parts, right, rops)


def solution(mesh):
    row_count, sec_count = mesh.shape["row"], mesh.shape["sec"]

    def on_device(left_block, right_block, left_ops, right_ops, charges, live_states, kept, start):
        left_all, arrived = exchange(row_count, sec_count, left_block, right_block)
        m, basis, part = chain(
            left_block.shape[0] * sec_count, left_all, arrived, left_ops, right_ops,
            charges, live_states, kept, start, left_block.shape[1],
        )
        m, parts = deliver(sec_count, m, part)
        return basis, finish(row_count, m, parts, right_block, right_ops)

    return jax.shard_map(
        on_device,
        mesh=mesh,
        in_specs=(P("sec", "row", None), P("sec", None, None), P(), P(), P(), P(), P(), P()),
        out_specs=(P("sec", "row", None), P("sec", None, "row")),
        check_vma=False,
    )
```

time: 527 us -> 119 us (0.23); the launches traced: 518 us -> 119 us
  waiting for transfers between devices: 222 us -> 0 us
  other arithmetic: 137 us -> 0 us
  Pallas kernels: 0 us -> 116 us
  matrix products: 77.8 us -> 0 us
  blocking collectives: 39 us -> 0 us
  local copies, waits for them, and re-layouts: 20.6 us -> 1.71 us
  between operations: 15.3 us -> 0.68 us
  starting transfers between devices: 6.72 us -> 0 us
    psum x3 -> x0, waiting for transfers between devices: 161 us -> none  [truncate(): lax.psum((jnp.einsum('sri,srj->sij', krylov, krylov, precision=highest),...]
    another operation x17 -> x0, other arithmetic: 131 us -> none  [the longest x10 71.1 us: truncate(): factor = jnp.linalg.cholesky(gram_matrix)]
    pallas_call x0 -> x4, Pallas kernels: none -> 116 us  [the longest x1 63.1 us: chain(): pl.pallas_call(functools.partial(chain_kernel, sector_count), out_shape=(...]
    dot_general x12 -> x0, matrix products: 65.6 us -> none  [the longest x2 31.1 us: truncate(): jnp.einsum('src,scj->srj', theta_block, projected, precision=highest)]
    ppermute x2 -> x0, waiting for transfers between devices: 60.2 us -> none  [from_partner(): return lax.ppermute(value, axis, pairs)]
    psum x1 -> x0, blocking collectives: 39 us -> none  [on_device(): total_weight = lax.psum(jnp.sum(right_part * right_part), ('sec', 'row'))]
    another operation x4 -> x0, matrix products: 12.2 us -> none  [single(): jax.scipy.linalg.solve_triangular(lower_factor, right_side.T, lower=True)]
    convert_element_type x4 -> x0, local copies, waits for them, and re-layouts: 11 us -> none  [the longest x2 9.99 us: gate_columns(): return mixed_columns.reshape(operators.shape[0] * tensor_block.shape[0],...]
  transfers between devices with their start and end apart: 5 -> 0, of which waited for: 5 -> 0; matrix products, arithmetic and copies ran while one was open for 2% -> 0% of each run, Pallas kernels for 0% -> 0%
where the time goes in v1:
time: 119 us
  Pallas kernels  116 us (97%)
  local copies, waits for them, and re-layouts  1.71 us (1%)
    pallas_call x1, Pallas kernels, chain(): pl.pallas_call(functools.partial(chain_kernel, sector_count), out_shape=(...  63.1 us
    pallas_call x1, Pallas kernels, exchange(): pl.pallas_call(functools.partial(exchange_kernel, row_count, sec_count //...  28 us
    pallas_call x1, Pallas kernels, deliver(): pl.pallas_call(functools.partial(deliver_kernel, sec_count), out_shape=(j...  19.7 us
    pallas_call x1, Pallas kernels, finish(): pl.pallas_call(functools.partial(finish_kernel, row_count), out_shape=jax...  5.43 us

profile of v1, /device:TPU:0, one launch (start us, length us, event | category | flops | bytes accessed | tf_op | source)
XLA Modules:
  0.0 118.6 jit_solution(6079897033890309934)
XLA Ops:
  0.6 28.0 %shard_map.95 = (bf16[2,2048,128]{2,1,0:T(8,128)(2,1)}, bf16[2,128,2048]{2,1,0:T(8,128)(2,1)}) custom-call(bf16[2,512,128]{2,1,0:T(8,128)(2,1)} %left_ref.1, bf16[2,128,2048]{2,1,0:T(8,128)(2,1)} %right_ref.3), custom_call_target="tpu_custom_call" | custom-call | tf_op jit(solution)/shard_map/pallas_call | solution.py:127
  28.7 0.0 copy-start
  28.7 63.1 %shard_map.96 = (bf16[2,512,128]{2,1,0:T(8,128)(2,1)}, f32[2,512,128]{2,1,0:T(8,128)}, f32[8,128]{1,0:T(8,128)}) custom-call(bf16[2,2048,128]{2,1,0:T(8,128)(2,1)} %get-tuple-element.9.left_ref, bf16[2,128,2048]{2,1,0:T(8,128)(2,1)} %get-tuple-element.10.right_ref, f32[4,16,16]{2,1,0:T(8,128)} %lops_ref.1, f32[4,16,16]{2,1,0:T(8,128)} %rops_ref.3, ...), custom_call_target="tpu_custom_call" | custom-call | tf_op jit(solution)/shard_map/pallas_call | solution.py:289
  91.8 0.0 copy-start.2
  91.8 19.7 %shard_map.97 = (bf16[2,512,128]{2,1,0:T(8,128)(2,1)}, f32[8,8,128]{2,1,0:T(8,128)}) custom-call(bf16[2,512,128]{2,1,0:T(8,128)(2,1)} %get-tuple-element.12.m_ref, f32[8,128]{1,0:T(8,128)} %get-tuple-element.13.part_ref), custom_call_target="tpu_custom_call" | custom-call | tf_op jit(solution)/shard_map/pallas_call | solution.py:341
  111.5 0.0 copy-done
  111.5 0.0 copy-done.2
  111.5 0.0 copy-start.1
  111.5 0.9 copy-done.1
  112.4 0.0 copy-start.3
  112.5 0.8 copy-done.3
  113.2 5.4 %shard_map.98 = f32[2,128,512]{2,1,0:T(8,128)} custom-call(bf16[2,512,128]{2,1,0:T(8,128)(2,1)S(1)} %copy-done.1, f32[8,8,128]{2,1,0:T(8,128)S(1)} %copy-done.3, bf16[2,128,2048]{2,1,0:T(8,128)(2,1)S(1)} %copy-done, f32[4,16,16]{2,1,0:T(8,128)S(1)} %copy-done.2), custom_call_target="tpu_custom_call" | custom-call | tf_op jit(solution)/shard_map/pallas_call | solution.py:397
Async XLA Ops:
  28.7 82.8 %copy-start = (bf16[2,128,2048]{2,1,0:T(8,128)(2,1)S(1)}, bf16[2,128,2048]{2,1,0:T(8,128)(2,1)}, u32[]{:S(2)}) copy-start(bf16[2,128,2048]{2,1,0:T(8,128)(2,1)} %right_ref.3) | copy-start | bytes 3145732
  91.8 19.7 %copy-start.2 = (f32[4,16,16]{2,1,0:T(8,128)S(1)}, f32[4,16,16]{2,1,0:T(8,128)}, u32[]{:S(2)}) copy-start(f32[4,16,16]{2,1,0:T(8,128)} %rops_ref.3) | copy-start | bytes 12292
  111.5 1.0 copy-start.1
  112.4 0.8 copy-start.3

commit v2 on v1

--- a/solution.py
+++ b/solution.py
@@ -13,6 +13,7 @@
 chemical = 0.4
 ITERS = 2
 PANEL = 16
+CHUNKS = 2
 VM = pl.BlockSpec(memory_space=pltpu.VMEM)
 SM = pl.BlockSpec(memory_space=pltpu.SMEM)
 
@@ -45,6 +46,19 @@
     rest = x - high.astype(F32)
     mid = rest.astype(BF16)
     return high, mid, (rest - mid.astype(F32)).astype(BF16)
+
+
+def presplit_nn(parts, x):
+    high, low = split2(x)
+    both = nn(parts[0], jnp.concatenate([high, low], axis=1))
+    width = x.shape[1]
+    return both[:, :width] + both[:, width:] + nn(parts[1], high)
+
+
+def nt3(a, b):
+    ah, al = split2(a)
+    bh, bl = split2(b)
+    return nt(jnp.concatenate([ah, al, ah], axis=1), jnp.concatenate([bh, bh, bl], axis=1))
 
 
 def iota(shape, dim):
@@ -73,8 +87,9 @@
     def left_at(owner):
         return left_out.at[:, pl.ds(pl.multiple_of(owner * rows, rows), rows), :]
 
-    def right_at(ref, owner):
-        return ref.at[:, pl.ds(pl.multiple_of(owner * depth, depth), depth), :]
+    def right_at(ref, owner, c):
+        size = depth // CHUNKS
+        return ref.at[:, pl.ds(pl.multiple_of(owner * depth + c * size, size), size), :]
 
     copies = []
 
@@ -95,7 +110,7 @@
             copy.wait_recv()
             taken.append(id(copy))
 
-    first = go(right_at(right_ref, row), right_at(right_out, row), partner)
+    pieces = [(row, c, go(*[right_at(ref, row, c) for ref in (right_ref, right_out)], partner)) for c in range(CHUNKS)]
     held = [(row, None)]
     for distance in distances:
         sent = []
@@ -108,14 +123,13 @@
         held = held + sent
     own = pl.ds(pl.multiple_of(row * rows, rows), rows)
     left_out[:, own, :] = left_ref[...]
-    held = [(row, first)]
     for distance in distances:
         sent = []
-        for owner, copy in held:
+        for owner, c, copy in pieces:
             arrive(copy)
-            block = right_at(right_out, owner)
-            sent.append((jnp.bitwise_xor(owner, distance), go(block, block, peer_row(distance))))
-        held = held + sent
+            block = right_at(right_out, owner, c)
+            sent.append((jnp.bitwise_xor(owner, distance), c, go(block, block, peer_row(distance))))
+        pieces = pieces + sent
     for copy in copies:
         copy.wait_send()
         arrive(copy)
@@ -123,7 +137,7 @@
 
 def exchange(row_count, sec_count, left, right):
     slots, rows, states = left.shape
-    count = 2 * (row_count - 1) + 1
+    count = row_count - 1 + CHUNKS * row_count
     return pl.pallas_call(
         functools.partial(exchange_kernel, row_count, sec_count // 2),
         out_shape=(
@@ -195,8 +209,8 @@
 
 def chain_kernel(
     sector_count, left_ref, right_ref, lops_ref, rops_ref, charges_ref, live_ref, kept_ref,
-    start_ref, m_out, u_out, part_out, at_ref, b_ref, kl_ref, kr_ref, ga_ref, gb_ref, s_ref,
-    t_ref,
+    start_ref, m_out, u_out, part_out, at_ref, b_ref, kl_ref, kr_ref, ga_ref, gah_ref, gal_ref, gbh_ref,
+    gbl_ref, s_ref, t_ref,
 ):
     slots, rows, states = left_ref.shape
     terms, site = lops_ref.shape[0], lops_ref.shape[1]
@@ -245,8 +259,10 @@
             return carry
 
         lax.fori_loop(0, states // group, right_chunk, 0)
-        ga_ref[s] = nt(at_ref[s], at_ref[s])
-        gb_ref[s] = nt(b_ref[s], b_ref[s])
+        gram = nt(at_ref[s], at_ref[s])
+        ga_ref[s] = gram
+        gah_ref[s], gal_ref[s] = split2(gram)
+        gbh_ref[s], gbl_ref[s] = split2(nt(b_ref[s], b_ref[s]))
 
     bond = terms * states
     weights = [
@@ -258,22 +274,26 @@
         wanted = start_ref[pl.ds(homes[s], 1), :]
         coef.append((iota((bond, wanted.shape[1]), 0) == wanted).astype(F32))
     for round_index in range(ITERS + 1):
-        image = [nn(ga_ref[s], coef[s], HIGHEST) for s in range(slots)]
+        if round_index < ITERS:
+            image = [presplit_nn((gah_ref[s], gal_ref[s]), coef[s]) for s in range(slots)]
+        else:
+            image = [nn(ga_ref[s], coef[s], HIGHEST) for s in range(slots)]
         inverse_factor([tn(coef[s], image[s], HIGHEST) for s in range(slots)], s_ref, t_ref)
-        image = [nt(image[s], t_ref[s], HIGHEST) for s in range(slots)]
+        image = [nt3(image[s], t_ref[s]) for s in range(slots)]
         if round_index < ITERS:
             coef = [
-                nn(gb_ref[s], image[s], HIGHEST) * (weights[s] * weights[s]) for s in range(slots)
+                presplit_nn((gbh_ref[s], gbl_ref[s]), image[s]) * (weights[s] * weights[s])
+                for s in range(slots)
             ]
         else:
-            coef = [nt(coef[s], t_ref[s], HIGHEST) for s in range(slots)]
+            coef = [nt3(coef[s], t_ref[s]) for s in range(slots)]
     local_rows = u_out.shape[1]
     total = jnp.zeros((8, states), F32)
     for s in range(slots):
         keep = iota((bond, coef[s].shape[1]), 1) < kept_ref[mirrors[s]]
         out = jnp.where(keep, image[s] * weights[s], 0.0)
         m_out[s] = out.astype(BF16)
-        per = out * nn(gb_ref[s], out, HIGHEST)
+        per = out * presplit_nn((gbh_ref[s], gbl_ref[s]), out)
         total = total + jnp.sum(per.reshape(bond // 8, 8, per.shape[1]), axis=0)
         high, low = split2(jnp.where(keep, coef[s], 0.0))
         here = at_ref[s, :, pl.ds(pl.multiple_of(row * local_rows, local_rows), local_rows)]
@@ -301,7 +321,10 @@
             pltpu.VMEM((2, block, terms * block), BF16),
             pltpu.VMEM((2, terms * block, block), BF16),
             pltpu.VMEM((slots, bond, bond), F32),
-            pltpu.VMEM((slots, bond, bond), F32),
+            pltpu.VMEM((slots, bond, bond), BF16),
+            pltpu.VMEM((slots, bond, bond), BF16),
+            pltpu.VMEM((slots, bond, bond), BF16),
+            pltpu.VMEM((slots, bond, bond), BF16),
             pltpu.VMEM((slots, keep, keep), F32),
             pltpu.VMEM((slots, keep, keep), F32),
         ],
@@ -309,15 +332,47 @@
     )(left, right, lops, rops, charges, live, kept, start)
 
 
-def deliver_kernel(sec_count, m_ref, part_ref, m_out, parts_out, m_send, m_recv, send, recv):
+def deliver_kernel(row_count, sec_count, m_ref, part_ref, m_out, parts_out, m_send, m_recv, send, recv):
     row, sec = lax.axis_index("row"), lax.axis_index("sec")
-    partner = (jnp.bitwise_xor(sec, sec_count // 2), row)
+    depth = m_ref.shape[1] // row_count
+    distances = []
+    step = row_count // 2
+    while step:
+        distances.append(step)
+        step //= 2
     barrier = pltpu.get_barrier_semaphore()
     for d in range(1, sec_count):
         pl.semaphore_signal(
             barrier, inc=1, device_id=(jnp.bitwise_xor(sec, d), row), device_id_type=MESH
         )
-    pl.semaphore_wait(barrier, sec_count - 1)
+    for d in distances:
+        pl.semaphore_signal(
+            barrier, inc=1, device_id=(sec, jnp.bitwise_xor(row, d)), device_id_type=MESH
+        )
+    pl.semaphore_wait(barrier, sec_count - 1 + len(distances))
+
+    def part_of(ref, owner):
+        return ref.at[:, pl.ds(pl.multiple_of(owner * depth, depth), depth), :]
+
+    copies, taken = [], []
+
+    def go(source, target, device):
+        index = len(copies)
+        copy = pltpu.make_async_remote_copy(
+            src_ref=source, dst_ref=target, send_sem=m_send.at[index], recv_sem=m_recv.at[index],
+            device_id=device, device_id_type=MESH,
+        )
+        copy.start()
+        copies.append(copy)
+        return copy
+
+    def arrive(copy):
+        if id(copy) not in taken:
+            copy.wait_recv()
+            taken.append(id(copy))
+
+    partner = (jnp.bitwise_xor(sec, sec_count // 2), row)
+    held = [(row, go(part_of(m_ref, row), part_of(m_out, row), partner))]
     small = []
     for d in range(1, sec_count):
         copy = pltpu.make_async_remote_copy(
@@ -326,20 +381,25 @@
         )
         copy.start()
         small.append(copy)
-    big = pltpu.make_async_remote_copy(
-        src_ref=m_ref, dst_ref=m_out, send_sem=m_send, recv_sem=m_recv, device_id=partner,
-        device_id_type=MESH,
-    )
-    big.start()
     parts_out[0] = part_ref[...]
+    for distance in distances:
+        sent = []
+        for owner, copy in held:
+            arrive(copy)
+            block = part_of(m_out, owner)
+            peer = (sec, jnp.bitwise_xor(row, distance))
+            sent.append((jnp.bitwise_xor(owner, distance), go(block, block, peer)))
+        held = held + sent
     for copy in small:
         copy.wait()
-    big.wait()
-
-
-def deliver(sec_count, m, part):
+    for copy in copies:
+        copy.wait_send()
+        arrive(copy)
+
+
+def deliver(row_count, sec_count, m, part):
     return pl.pallas_call(
-        functools.partial(deliver_kernel, sec_count),
+        functools.partial(deliver_kernel, row_count, sec_count),
         out_shape=(
             jax.ShapeDtypeStruct(m.shape, m.dtype),
             jax.ShapeDtypeStruct((sec_count,) + part.shape, part.dtype),
@@ -347,8 +407,8 @@
         in_specs=[VM] * 2,
         out_specs=[VM] * 2,
         scratch_shapes=[
-            pltpu.SemaphoreType.DMA,
-            pltpu.SemaphoreType.DMA,
+            pltpu.SemaphoreType.DMA((row_count,)),
+            pltpu.SemaphoreType.DMA((row_count,)),
             pltpu.SemaphoreType.DMA((sec_count,)),
             pltpu.SemaphoreType.DMA((sec_count,)),
         ],
@@ -416,7 +476,7 @@
             left_block.shape[0] * sec_count, left_all, arrived, left_ops, right_ops,
             charges, live_states, kept, start, left_block.shape[1],
         )
-        m, parts = deliver(sec_count, m, part)
+        m, parts = deliver(row_count, sec_count, m, part)
         return basis, finish(row_count, m, parts, right_block, right_ops)
 
     return jax.shard_map(

time: 119 us -> 105 us (0.88)
  Pallas kernels: 116 us -> 102 us
    pallas_call x1, Pallas kernels: 63.1 us -> 56.2 us  [chain(): pl.pallas_call(functools.partial(chain_kernel, sector_count), out_shape=(...]
    pallas_call x1, Pallas kernels: 19.7 us -> 14.6 us  [deliver(): pl.pallas_call(functools.partial(deliver_kernel, row_count, sec_count), o...]
    pallas_call x1, Pallas kernels: 28 us -> 25.7 us  [exchange(): pl.pallas_call(functools.partial(exchange_kernel, row_count, sec_count //...]
where the time goes in v2:
time: 105 us; the launch traced here: 104 us
  Pallas kernels  102 us (97%)
  local copies, waits for them, and re-layouts  1.71 us (2%)
    pallas_call x1, Pallas kernels, chain(): pl.pallas_call(functools.partial(chain_kernel, sector_count), out_shape=(...  56.2 us
    pallas_call x1, Pallas kernels, exchange(): pl.pallas_call(functools.partial(exchange_kernel, row_count, sec_count //...  25.7 us
    pallas_call x1, Pallas kernels, deliver(): pl.pallas_call(functools.partial(deliver_kernel, row_count, sec_count), o...  14.6 us
    pallas_call x1, Pallas kernels, finish(): pl.pallas_call(functools.partial(finish_kernel, row_count), out_shape=jax...  5.43 us

profile of v2, /device:TPU:0, one launch (start us, length us, event | category | flops | bytes accessed | tf_op | source)
XLA Modules:
  0.0 104.4 jit_solution(12002919440050788281)
XLA Ops:
  0.6 25.7 %shard_map.95 = (bf16[2,2048,128]{2,1,0:T(8,128)(2,1)}, bf16[2,128,2048]{2,1,0:T(8,128)(2,1)}) custom-call(bf16[2,512,128]{2,1,0:T(8,128)(2,1)} %left_ref.1, bf16[2,128,2048]{2,1,0:T(8,128)(2,1)} %right_ref.3), custom_call_target="tpu_custom_call" | custom-call | tf_op jit(solution)/shard_map/pallas_call | solution.py:141
  26.3 0.0 copy-start
  26.3 56.2 %shard_map.96 = (bf16[2,512,128]{2,1,0:T(8,128)(2,1)}, f32[2,512,128]{2,1,0:T(8,128)}, f32[8,128]{1,0:T(8,128)}) custom-call(bf16[2,2048,128]{2,1,0:T(8,128)(2,1)} %get-tuple-element.9.left_ref, bf16[2,128,2048]{2,1,0:T(8,128)(2,1)} %get-tuple-element.10.right_ref, f32[4,16,16]{2,1,0:T(8,128)} %lops_ref.1, f32[4,16,16]{2,1,0:T(8,128)} %rops_ref.3, ...), custom_call_target="tpu_custom_call" | custom-call | tf_op jit(solution)/shard_map/pallas_call | solution.py:309
  82.6 0.0 copy-start.2
  82.6 14.6 %shard_map.97 = (bf16[2,512,128]{2,1,0:T(8,128)(2,1)}, f32[8,8,128]{2,1,0:T(8,128)}) custom-call(bf16[2,512,128]{2,1,0:T(8,128)(2,1)} %get-tuple-element.12.m_ref, f32[8,128]{1,0:T(8,128)} %get-tuple-element.13.part_ref), custom_call_target="tpu_custom_call" | custom-call | tf_op jit(solution)/shard_map/pallas_call | solution.py:401
  97.2 0.0 copy-done
  97.2 0.0 copy-done.2
  97.2 0.0 copy-start.1
  97.3 0.9 copy-done.1
  98.2 0.0 copy-start.3
  98.2 0.8 copy-done.3
  99.0 5.4 %shard_map.98 = f32[2,128,512]{2,1,0:T(8,128)} custom-call(bf16[2,512,128]{2,1,0:T(8,128)(2,1)S(1)} %copy-done.1, f32[8,8,128]{2,1,0:T(8,128)S(1)} %copy-done.3, bf16[2,128,2048]{2,1,0:T(8,128)(2,1)S(1)} %copy-done, f32[4,16,16]{2,1,0:T(8,128)S(1)} %copy-done.2), custom_call_target="tpu_custom_call" | custom-call | tf_op jit(solution)/shard_map/pallas_call | solution.py:457
Async XLA Ops:
  26.3 70.9 %copy-start = (bf16[2,128,2048]{2,1,0:T(8,128)(2,1)S(1)}, bf16[2,128,2048]{2,1,0:T(8,128)(2,1)}, u32[]{:S(2)}) copy-start(bf16[2,128,2048]{2,1,0:T(8,128)(2,1)} %right_ref.3) | copy-start | bytes 3145732
  82.6 14.7 %copy-start.2 = (f32[4,16,16]{2,1,0:T(8,128)S(1)}, f32[4,16,16]{2,1,0:T(8,128)}, u32[]{:S(2)}) copy-start(f32[4,16,16]{2,1,0:T(8,128)} %rops_ref.3) | copy-start | bytes 12292
  97.2 1.0 copy-start.1
  98.2 0.8 copy-start.3
